TPU v7x, 256 devices: a whole 4x4x8 slice. The times are simulated.
256 devices in a mesh: sec: 2 (over y_hi), col: 8 (over z), row: 16 (over y_lo, x, core).
Axes of the slice: x: 4, y: 4 (y_hi: 2, y_lo: 2; y = y_hi * 2 + y_lo), z: 8, core: 2. Of those that a mesh axis runs over, the one named last changes fastest.
Arguments:
- ancestor: float32 [16384, 16384], P('row', ('sec', 'col')), may hold values from -0.3 to 0.3
- panel: float32 [2, 8192, 2048], P('sec', 'row', 'col'), may hold values from -1.5 to 1.5
- diag_inverse: float32 [2, 2048, 2048], P('sec', 'col', 'row'), may hold values from -12 to 12
- frontier: int32 [2, 16, 4], replicated, may hold values from 0 to 7, as said below
- counts: int32 [2, 16], replicated, may hold values from 1 to 4
- pattern: int32 [2, 64, 64], replicated, may hold values 0 or 1
Outputs:
- cross_block: float32 [2, 2048, 8192], P('sec', 'col', 'row')
- inverse: float32 [2, 2048, 2048], P('sec', 'col', 'row')
Inputs may be any that keep to these rules, and one draw needn't show every extreme that they name: The 4 offsets of one child and group are distinct; slot j of group g is ancestor tile 8 * g + frontier[c, g, j]. Slots j >= counts[c, g] of group g are padding for child c.
All inputs are finite; a program needn't handle non-finite values.
Results may differ from a plain program's by a relative error of at most 0.0001.
Values sent between devices are 32-bit elements; how exact they have to be, the bound alone decides.
No kernel may reach another device: no remote copies, remote signals or barrier semaphores. Data moves between devices by JAX's collectives and lax.ppermute only.
A program may use at most 128 MiB of HBM per device.

v0:
```python
import jax
import jax.numpy as jnp
from jax import lax
from jax.sharding import PartitionSpec as P

TILE = 128
GROUP = 8
SLOTS = 4


def swapped(value, axis, distance):
    mask = 2**distance
    pairs = [(source, source ^ mask) for source in range(lax.axis_size(axis))]
    return lax.ppermute(value, axis, pairs)


def from_root(value, axis, source):
    kept = jnp.where(lax.axis_index(axis) == source, value, 0).astype(value.dtype)
    return lax.psum(kept, axis)


def cut_along(value, dim, devices):
    before, after = (value.shape[:dim], value.shape[dim + 1 :])
    return jnp.moveaxis(value.reshape(*before, devices, -1, *after), dim, 0)


def summed_on_arrival(value, axis, dim):
    devices = lax.axis_size(axis)
    blocks = lax.all_to_all(cut_along(value, dim, devices), axis, 0, 0, tiled=True)
    return jnp.sum(blocks, axis=0)


def pick_tiles(
    ancestor, frontier, counts, pattern, child_id, row_start, block_start, row_groups, block_groups
):
    offsets = lax.dynamic_index_in_dim(frontier, child_id, 0, keepdims=False)
    sizes_live = lax.dynamic_index_in_dim(counts, child_id, 0, keepdims=False)
    pattern_child = lax.dynamic_index_in_dim(pattern, child_id, 0, keepdims=False)
    slot_ids = jnp.arange(SLOTS, dtype=jnp.int32)
    alive_slots = (slot_ids[None, :] < sizes_live[:, None]).astype(jnp.float32)
    within = jnp.arange(TILE, dtype=jnp.int32)
    row_offsets = lax.dynamic_slice_in_dim(offsets, row_start, row_groups, 0)
    col_offsets = lax.dynamic_slice_in_dim(offsets, block_start, block_groups, 0)
    row_tiles = (jnp.arange(row_groups, dtype=jnp.int32)[:, None] * GROUP + row_offsets).reshape(-1)
    col_tiles = (jnp.arange(block_groups, dtype=jnp.int32)[:, None] * GROUP + col_offsets).reshape(
        -1
    )
    row_indices = (row_tiles[:, None] * TILE + within[None, :]).reshape(-1)
    col_indices = (col_tiles[:, None] * TILE + within[None, :]).reshape(-1)
    picked = jnp.take(jnp.take(ancestor, row_indices, axis=0), col_indices, axis=1)
    row_alive = lax.dynamic_slice_in_dim(alive_slots, row_start, row_groups, 0).reshape(-1)
    col_alive = lax.dynamic_slice_in_dim(alive_slots, block_start, block_groups, 0).reshape(-1)
    row_slots = row_groups * SLOTS
    col_slots = block_groups * SLOTS
    pattern_block = lax.dynamic_slice(
        pattern_child, (row_start * SLOTS, block_start * SLOTS), (row_slots, col_slots)
    ).astype(jnp.float32)
    tile_mask = pattern_block * row_alive[:, None] * col_alive[None, :]
    shaped = picked.reshape(row_slots, TILE, col_slots, TILE) * tile_mask[:, None, :, None]
    return shaped.reshape(row_slots * TILE, col_slots * TILE)


def per_device(ancestor, panel, diag_inverse, frontier, counts, pattern):
    sec_index = lax.axis_index("sec")
    row_index = lax.axis_index("row")
    col_index = lax.axis_index("col")
    row_count = lax.axis_size("row")
    col_count = lax.axis_size("col")
    groups_all = frontier.shape[1]
    row_groups = groups_all // row_count
    block_groups = groups_all // (2 * col_count)
    own_block = sec_index * col_count + col_index
    row_start = row_index * row_groups
    block_start = own_block * block_groups
    mine = pick_tiles(
        ancestor,
        frontier,
        counts,
        pattern,
        sec_index,
        row_start,
        block_start,
        row_groups,
        block_groups,
    )
    theirs = pick_tiles(
        ancestor,
        frontier,
        counts,
        pattern,
        1 - sec_index,
        row_start,
        block_start,
        row_groups,
        block_groups,
    )
    partner = swapped(theirs, "sec", 0)
    leading = jnp.where(sec_index == 0, mine, partner)
    trailing = jnp.where(sec_index == 0, partner, mine)
    chosen = jnp.concatenate([leading, trailing], axis=1)
    rows_full = lax.all_gather(panel[0], "col", axis=1, tiled=True)
    starts = []
    for block_id in (col_index, col_count + col_index):
        starts.append(block_id * block_groups + 0)
    pieces = []
    for first_group in starts:
        received = from_root(rows_full, "row", first_group // row_groups)
        pieces.append(received)
    columns = jnp.concatenate(pieces, axis=0)
    cross_part = -lax.psum_scatter(
        lax.dot_general(
            columns,
            chosen,
            (((0,), (1,)), ((), ())),
            precision=lax.Precision.HIGHEST,
            preferred_element_type=jnp.float32,
        ),
        "col",
        scatter_dimension=0,
        tiled=True,
    )
    products = jnp.dot(
        cross_part, rows_full, precision=lax.Precision.HIGHEST, preferred_element_type=jnp.float32
    )
    summed = summed_on_arrival(products, "row", 1)
    inverse_part = diag_inverse[0] - summed
    return (cross_part[None], inverse_part[None])


def solution(mesh):
    return jax.shard_map(
        per_device,
        mesh=mesh,
        in_specs=(
            P("row", ("sec", "col")),
            P("sec", "row", "col"),
            P("sec", "col", "row"),
            P(),
            P(),
            P(),
        ),
        out_specs=(P("sec", "col", "row"), P("sec", "col", "row")),
        check_vma=False,
    )
```

profile of v0, /device:TPU:3, one launch (start us, length us, event | category | flops | bytes accessed | tf_op | source)
XLA Modules:
  0.0 345.1 jit_solution(13691169401568355810)
XLA Ops:
  7.2 0.7 all-gather.3.cloned.1.call-update
  8.0 59.4 %all-gather.3.cloned.1.call-done = f32[1,512,2048]{2,1,0:T(8,128)} async-done(((f32[1,512,256]{2,1,0:T(8,128)}), f32[1,512,2048]{2,1,0:T(8,128)}) %all-gather.3.cloned.1.call-update) | async-done | bytes 4194320 | tf_op jit(solution)/shard_map/all_gather | solution.py:101
  67.3 6.8 %bitcast_select_fusion.1 = (f32[512,2048]{1,0:T(8,128)}, f32[512,2048]{1,0:T(8,128)}) fusion(f32[1,512,2048]{2,1,0:T(8,128)} %all-gather.3.cloned.1.call-done, pred[]{:T(512)S(6)} %eq.10, pred[]{:T(512)S(6)} %eq.11), kind=kLoop, calls=%fused_computation.11 | loop fusion | flops 2097152 | bytes 12582914 | tf_op jit(solution)/shard_map/jit(_where)/select_n | solution.py:18
  74.9 0.8 fusion.24
  76.1 5.0 %gather_fusion.2 = f32[512,1024]{1,0:T(8,128)S(1)} fusion(f32[1024,1024]{1,0:T(8,128)} %param.10, s32[1024]{0:T(1024)S(1)} %pad_clamp_fusion.1), kind=kCustom, calls=%fused_computation.2.clone | custom fusion | bytes 4196352 | tf_op jit(solution)/shard_map/jit(_take)/gather | solution.py:50
  81.2 1.5 broadcast_select_fusion
  82.7 1.9 copy.14
  84.7 1.6 gather_fusion.3
  86.5 1.2 bitcast_multiply_fusion
  87.7 2.7 collective-permute-start
  90.6 5.1 %gather_fusion = f32[512,1024]{1,0:T(8,128)S(1)} fusion(f32[1024,1024]{1,0:T(8,128)} %param.10, s32[1024]{0:T(1024)S(1)} %pad_clamp_fusion.3), kind=kCustom, calls=%fused_computation.clone | custom fusion | bytes 4196352 | tf_op jit(solution)/shard_map/jit(_take)/gather | solution.py:50
  95.8 1.5 broadcast_select_fusion.1
  97.3 1.9 copy.12
  99.3 1.6 gather_fusion.1
  100.9 12.5 %collective-permute-done = f32[512,512]{0,1:T(8,128)} collective-permute-done((f32[512,512]{0,1:T(8,128)}, f32[512,512]{0,1:T(8,128)}, u32[]{:S(2)}, u32[]{:S(2)}) %collective-permute-start) | collective-permute-done | bytes 1048608 | tf_op jit(solution)/shard_map/ppermute | solution.py:14
  113.6 1.5 broadcast_select_fusion.3
  115.1 103.7 %all-reduce.3.cloned.1.call-done = (f32[512,2048]{1,0:T(8,128)}, f32[512,2048]{1,0:T(8,128)}) async-done(((f32[512,2048]{1,0:T(8,128)}, f32[512,2048]{1,0:T(8,128)}), (f32[512,2048]{1,0:T(8,128)}, f32[512,2048]{1,0:T(8,128)})) %all-reduce.3.cloned.1.call-update) | async-done | bytes 8388624 | tf_op jit(solution)/shard_map/psum | solution.py:19
  218.8 16.6 %fusion = f32[2048,512]{1,0:T(8,128)} fusion(f32[512,2048]{1,0:T(8,128)} %get-tuple-element.8, f32[512,2048]{1,0:T(8,128)} %get-tuple-element.9, f32[512,512]{0,1:T(8,128)S(1)} %get-tuple-element.13, f32[512,512]{0,1:T(8,128)S(1)} %get-tuple-element.12), kind=kOutput, calls=%fused_computation.4 | convolution fusion | flops 12887523328 | bytes 14680064 | tf_op jit(solution)/shard_map/dot_general | solution.py:111
  235.4 60.8 %reduce-scatter.2.cloned.1.call-done = f32[256,512]{1,0:T(8,128)} async-done(((f32[2048,512]{1,0:T(8,128)}), f32[256,512]{1,0:T(8,128)}) %reduce-scatter.2.cloned.1.call-update) | async-done | bytes 524304 | tf_op jit(solution)/shard_map/reduce_scatter | solution.py:110
  296.1 5.5 %fusion.9 = f32[32,16,8,128]{3,2,1,0:T(8,128)S(1)} fusion(f32[1,512,2048]{2,1,0:T(8,128)} %all-gather.3.cloned.1.call-done, f32[256,512]{1,0:T(8,128)} %reduce-scatter.2.cloned.1.call-done), kind=kOutput, calls=%fused_computation.16 | convolution fusion | flops 3221356544 | bytes 6815744 | tf_op jit(solution)/shard_map/dot_general | solution.py:122
  301.7 1.6 copy.27
  303.2 6.2 %all-to-all-start = ((f32[16,256,128]{2,1,0:T(8,128)}), f32[16,256,128]{2,1,0:T(8,128)S(1)}, u32[]{:S(2)}, u32[]{:S(2)}) async-start(f32[16,256,128]{2,1,0:T(8,128)} %bitcast.79), calls=%async_computation.1 | async-start | bytes 4194304 | tf_op jit(solution)/shard_map/all_to_all | solution.py:29
  309.5 0.8 negate_bitcast_fusion
  310.3 27.5 %all-to-all-done = f32[16,256,128]{2,1,0:T(8,128)S(1)} async-done(((f32[16,256,128]{2,1,0:T(8,128)}), f32[16,256,128]{2,1,0:T(8,128)S(1)}, u32[]{:S(2)}, u32[]{:S(2)}) %all-to-all-start) | async-done | bytes 2097184 | tf_op jit(solution)/shard_map/all_to_all | solution.py:29
  (32 shorter events, 2.8 us)
Async XLA Ops:
  7.2 60.2 %all-gather.3.cloned.1.call-start = ((), (), s32[]{:S(2)}) async-start(), calls=%async_computation.3 | async-start | bytes 4718592 | tf_op jit(solution)/shard_map/all_gather | solution.py:101
  7.9 210.9 %all-reduce.3.cloned.1.call-start = ((), (), s32[]{:S(2)}) async-start(), calls=%async_computation.4 | async-start | bytes 16777216 | tf_op jit(solution)/shard_map/psum | solution.py:19
  74.1 0.7 copy-start.3
  74.1 1.7 copy-start.2
  74.1 222.0 %reduce-scatter.2.cloned.1.call-start = ((), (), s32[]{:S(2)}) async-start(), calls=%async_computation.2 | async-start | bytes 4718592 | tf_op jit(solution)/shard_map/reduce_scatter | solution.py:110
  87.7 25.7 %collective-permute-start = (f32[512,512]{0,1:T(8,128)}, f32[512,512]{0,1:T(8,128)}, u32[]{:S(2)}, u32[]{:S(2)}) collective-permute-start(f32[512,512]{0,1:T(8,128)} %bitcast_multiply_fusion), channel_id=1, source_target_pairs={{0,128},{128,0},{1,129},{129,1},{2,130},{130,2},{3,131},{131,3},{4... | collective-permute-start | bytes 3145736 | tf_op jit(solution)/shard_map/ppermute | solution.py:14
  303.2 6.2 %copy-start = (f32[256,512]{1,0:T(8,128)S(1)}, f32[256,512]{1,0:T(8,128)}, u32[]{:S(2)}) copy-start(f32[256,512]{1,0:T(8,128)} %reduce-scatter.2.cloned.1.call-done) | copy-start | bytes 1572868
  303.2 34.6 %all-to-all-start = ((f32[16,256,128]{2,1,0:T(8,128)}), f32[16,256,128]{2,1,0:T(8,128)S(1)}, u32[]{:S(2)}, u32[]{:S(2)}) async-start(f32[16,256,128]{2,1,0:T(8,128)} %bitcast.79), calls=%async_computation.1 | async-start | bytes 4194304 | tf_op jit(solution)/shard_map/all_to_all | solution.py:29
  309.5 28.5 %copy-start.1 = (f32[1,256,128]{2,1,0:T(8,128)S(1)}, f32[1,256,128]{2,1,0:T(8,128)}, u32[]{:S(2)}) copy-start(f32[1,256,128]{2,1,0:T(8,128)} %param.12) | copy-start | bytes 393220
Sparse Core Ops, SparseCore 0:
  9.8 57.5 all-gather.2
  74.3 144.4 all-reduce.2
  235.5 60.5 reduce-scatter.1
where the time goes:
time: 346 us; the launch traced here: 345 us
  waiting for transfers between devices  265 us (77%)
  matrix products  22.1 us (6%)
  local copies, waits for them, and re-layouts  20 us (6%)
  other arithmetic  15.5 us (4%)
  between operations  13.9 us (4%)
  starting transfers between devices  9.09 us (3%)
    psum x1, waiting for transfers between devices, from_root(): return lax.psum(kept, axis)  104 us
    reduce_scatter x1, waiting for transfers between devices, per_device(): lax.psum_scatter(lax.dot_general(columns, chosen, (((0,), (1,)), ((), ())...  60.8 us
    all_gather x1, waiting for transfers between devices, per_device(): rows_full = lax.all_gather(panel[0], 'col', axis=1, tiled=True)  59.4 us
    all_to_all x1, waiting for transfers between devices, summed_on_arrival(): lax.all_to_all(cut_along(value, dim, devices), axis, 0, 0, tiled=True)  27.5 us
    dot_general x1, matrix products, per_device(): lax.dot_general(columns, chosen, (((0,), (1,)), ((), ())), precision=lax....  16.6 us
    ppermute x1, waiting for transfers between devices, swapped(): return lax.ppermute(value, axis, pairs)  12.5 us
    gather x2, local copies, waits for them, and re-layouts, pick_tiles(): jnp.take(ancestor, row_indices, axis=0)  10.1 us
  transfers between devices with their start and end apart: 5, of which 5 were waited for; matrix products, arithmetic and copies ran while one was open for 7% of the time, Pallas kernels for 0%

commit v1 on v0

--- a/solution.py
+++ b/solution.py
@@ -98,7 +98,9 @@
     leading = jnp.where(sec_index == 0, mine, partner)
     trailing = jnp.where(sec_index == 0, partner, mine)
     chosen = jnp.concatenate([leading, trailing], axis=1)
-    rows_full = lax.all_gather(panel[0], "col", axis=1, tiled=True)
+    rows_full = jnp.concatenate(
+        lax.all_to_all(jnp.stack([panel[0]] * lax.axis_size("col")), "col", 0, 0), axis=1
+    )
     starts = []
     for block_id in (col_index, col_count + col_index):
         starts.append(block_id * block_groups + 0)

time: 346 us -> 391 us (1.13)
  waiting for transfers between devices: 265 us -> 298 us
  starting transfers between devices: 9.09 us -> 17.4 us
    all_to_all x0 -> x1, waiting for transfers between devices: none -> 96.8 us  [per_device(): lax.all_to_all(jnp.stack([panel[0]] * lax.axis_size('col')), 'col', 0, 0)]
    all_gather x1 -> x0, waiting for transfers between devices: 59.4 us -> none  [per_device(): rows_full = lax.all_gather(panel[0], 'col', axis=1, tiled=True)]
    all_to_all x0 -> x1, starting transfers between devices: none -> 8.19 us  [per_device(): lax.all_to_all(jnp.stack([panel[0]] * lax.axis_size('col')), 'col', 0, 0)]
where the time goes in v1:
time: 391 us
  waiting for transfers between devices  298 us (76%)
  matrix products  23.2 us (6%)
  local copies, waits for them, and re-layouts  22.1 us (6%)
  starting transfers between devices  17.4 us (4%)
  other arithmetic  15.5 us (4%)
  between operations  14.2 us (4%)
    psum x1, waiting for transfers between devices, from_root(): return lax.psum(kept, axis)  100 us
    all_to_all x1, waiting for transfers between devices, per_device(): lax.all_to_all(jnp.stack([panel[0]] * lax.axis_size('col')), 'col', 0, 0)  96.8 us
    reduce_scatter x1, waiting for transfers between devices, per_device(): lax.psum_scatter(lax.dot_general(columns, chosen, (((0,), (1,)), ((), ())...  60.8 us
    all_to_all x1, waiting for transfers between devices, summed_on_arrival(): lax.all_to_all(cut_along(value, dim, devices), axis, 0, 0, tiled=True)  27.5 us
    dot_general x1, matrix products, per_device(): lax.dot_general(columns, chosen, (((0,), (1,)), ((), ())), precision=lax....  16.6 us
    ppermute x1, waiting for transfers between devices, swapped(): return lax.ppermute(value, axis, pairs)  12.7 us
    gather x2, local copies, waits for them, and re-layouts, pick_tiles(): jnp.take(ancestor, row_indices, axis=0)  10 us
    all_to_all x1, starting transfers between devices, per_device(): lax.all_to_all(jnp.stack([panel[0]] * lax.axis_size('col')), 'col', 0, 0)  8.19 us
  transfers between devices with their start and end apart: 5, of which 5 were waited for; matrix products, arithmetic and copies ran while one was open for 7% of the time, Pallas kernels for 0%

profile of v1, /device:TPU:3, one launch (start us, length us, event | category | flops | bytes accessed | tf_op | source)
XLA Modules:
  0.0 390.5 jit_solution(15972735812021151962)
XLA Ops:
  7.2 1.2 copy.8
  8.4 2.5 stack.3
  10.9 8.2 %all-to-all-start = ((f32[8,512,256]{1,2,0:T(8,128)}), f32[8,512,256]{1,2,0:T(8,128)}, u32[]{:S(2)}, u32[]{:S(2)}) async-start(f32[8,512,256]{1,2,0:T(8,128)} %stack.3), calls=%async_computation | async-start | bytes 8388608 | tf_op jit(solution)/shard_map/all_to_all | solution.py:102
  19.2 96.8 %all-to-all-done = f32[8,512,256]{1,2,0:T(8,128)} async-done(((f32[8,512,256]{1,2,0:T(8,128)}), f32[8,512,256]{1,2,0:T(8,128)}, u32[]{:S(2)}, u32[]{:S(2)}) %all-to-all-start) | async-done | bytes 4194336 | tf_op jit(solution)/shard_map/all_to_all | solution.py:102
  116.0 6.7 %bitcast_select_fusion.1 = (f32[512,2048]{0,1:T(8,128)}, f32[512,2048]{0,1:T(8,128)}) fusion(f32[8,512,256]{1,2,0:T(8,128)} %all-to-all-done, pred[]{:T(512)S(6)} %eq.10, pred[]{:T(512)S(6)} %eq.11), kind=kLoop, calls=%fused_computation.9 | loop fusion | flops 2097152 | bytes 12582914 | tf_op jit(solution)/shard_map/jit(_where)/select_n | solution.py:18
  124.7 5.0 %gather_fusion.2 = f32[512,1024]{1,0:T(8,128)S(1)} fusion(f32[1024,1024]{1,0:T(8,128)} %param.10, s32[1024]{0:T(1024)S(1)} %pad_clamp_fusion.1), kind=kCustom, calls=%fused_computation.2.clone | custom fusion | bytes 4196352 | tf_op jit(solution)/shard_map/jit(_take)/gather | solution.py:50
  129.8 1.5 broadcast_select_fusion
  131.3 1.9 copy.11
  133.3 1.6 gather_fusion.3
  135.1 1.2 bitcast_multiply_fusion
  136.3 2.9 collective-permute-start
  139.4 5.0 %gather_fusion = f32[512,1024]{1,0:T(8,128)S(1)} fusion(f32[1024,1024]{1,0:T(8,128)} %param.10, s32[1024]{0:T(1024)S(1)} %pad_clamp_fusion.3), kind=kCustom, calls=%fused_computation.clone | custom fusion | bytes 4196352 | tf_op jit(solution)/shard_map/jit(_take)/gather | solution.py:50
  144.5 1.5 broadcast_select_fusion.1
  146.0 1.9 copy.9
  148.0 1.6 gather_fusion.1
  149.6 12.7 %collective-permute-done = f32[512,512]{0,1:T(8,128)} collective-permute-done((f32[512,512]{0,1:T(8,128)}, f32[512,512]{0,1:T(8,128)}, u32[]{:S(2)}, u32[]{:S(2)}) %collective-permute-start) | collective-permute-done | bytes 1048608 | tf_op jit(solution)/shard_map/ppermute | solution.py:14
  162.5 1.5 broadcast_select_fusion.3
  164.0 100.3 %all-reduce.3.cloned.1.call-done = (f32[512,2048]{0,1:T(8,128)}, f32[512,2048]{0,1:T(8,128)}) async-done(((f32[512,2048]{0,1:T(8,128)}, f32[512,2048]{0,1:T(8,128)}), (f32[512,2048]{0,1:T(8,128)}, f32[512,2048]{0,1:T(8,128)})) %all-reduce.3.cloned.1.call-update) | async-done | bytes 8388624 | tf_op jit(solution)/shard_map/psum | solution.py:19
  264.3 16.6 %fusion = f32[2048,512]{1,0:T(8,128)} fusion(f32[512,2048]{0,1:T(8,128)} %get-tuple-element.8, f32[512,2048]{0,1:T(8,128)} %get-tuple-element.9, f32[512,512]{0,1:T(8,128)S(1)} %get-tuple-element.13, f32[512,512]{0,1:T(8,128)S(1)} %get-tuple-element.12), kind=kOutput, calls=%fused_computation.4 | convolution fusion | flops 12887523328 | bytes 14680064 | tf_op jit(solution)/shard_map/dot_general | solution.py:113
  281.0 60.8 %reduce-scatter.2.cloned.1.call-done = f32[256,512]{1,0:T(8,128)} async-done(((f32[2048,512]{1,0:T(8,128)}), f32[256,512]{1,0:T(8,128)}) %reduce-scatter.2.cloned.1.call-update) | async-done | bytes 524304 | tf_op jit(solution)/shard_map/reduce_scatter | solution.py:112
  341.8 6.6 %convolution_bitcast_fusion = f32[16,256,128]{2,1,0:T(8,128)} fusion(f32[16,128,512]{2,1,0:T(8,128)} %bitcast.21, f32[256,512]{1,0:T(8,128)} %reduce-scatter.2.cloned.1.call-done), kind=kOutput, calls=%fused_computation.13 | convolution fusion | flops 3221356544 | bytes 6815744 | tf_op jit(solution)/shard_map/dot_general | solution.py:124
  348.3 6.2 %all-to-all-start.1 = ((f32[16,256,128]{2,1,0:T(8,128)}), f32[16,256,128]{2,1,0:T(8,128)S(1)}, u32[]{:S(2)}, u32[]{:S(2)}) async-start(f32[16,256,128]{2,1,0:T(8,128)} %convolution_bitcast_fusion), calls=%async_computation.2 | async-start | bytes 4194304 | tf_op jit(solution)/shard_map/all_to_all | solution.py:29
  354.6 0.8 negate_bitcast_fusion
  355.4 27.5 %all-to-all-done.1 = f32[16,256,128]{2,1,0:T(8,128)S(1)} async-done(((f32[16,256,128]{2,1,0:T(8,128)}), f32[16,256,128]{2,1,0:T(8,128)S(1)}, u32[]{:S(2)}, u32[]{:S(2)}) %all-to-all-start.1) | async-done | bytes 2097184 | tf_op jit(solution)/shard_map/all_to_all | solution.py:29
  (32 shorter events, 3.5 us)
Async XLA Ops:
  10.9 105.0 %all-to-all-start = ((f32[8,512,256]{1,2,0:T(8,128)}), f32[8,512,256]{1,2,0:T(8,128)}, u32[]{:S(2)}, u32[]{:S(2)}) async-start(f32[8,512,256]{1,2,0:T(8,128)} %stack.3), calls=%async_computation | async-start | bytes 8388608 | tf_op jit(solution)/shard_map/all_to_all | solution.py:102
  19.1 245.2 %all-reduce.3.cloned.1.call-start = ((), (), s32[]{:S(2)}) async-start(), calls=%async_computation.4 | async-start | bytes 16777216 | tf_op jit(solution)/shard_map/psum | solution.py:19
  122.7 0.7 copy-start.3
  122.7 1.7 copy-start.2
  122.7 219.1 %reduce-scatter.2.cloned.1.call-start = ((), (), s32[]{:S(2)}) async-start(), calls=%async_computation.3 | async-start | bytes 4718592 | tf_op jit(solution)/shard_map/reduce_scatter | solution.py:112
  136.3 26.1 %collective-permute-start = (f32[512,512]{0,1:T(8,128)}, f32[512,512]{0,1:T(8,128)}, u32[]{:S(2)}, u32[]{:S(2)}) collective-permute-start(f32[512,512]{0,1:T(8,128)} %bitcast_multiply_fusion), channel_id=1, source_target_pairs={{0,128},{128,0},{1,129},{129,1},{2,130},{130,2},{3,131},{131,3},{4... | collective-permute-start | bytes 3145736 | tf_op jit(solution)/shard_map/ppermute | solution.py:14
  348.3 6.2 %copy-start = (f32[256,512]{1,0:T(8,128)S(1)}, f32[256,512]{1,0:T(8,128)}, u32[]{:S(2)}) copy-start(f32[256,512]{1,0:T(8,128)} %reduce-scatter.2.cloned.1.call-done) | copy-start | bytes 1572868
  348.3 34.6 %all-to-all-start.1 = ((f32[16,256,128]{2,1,0:T(8,128)}), f32[16,256,128]{2,1,0:T(8,128)S(1)}, u32[]{:S(2)}, u32[]{:S(2)}) async-start(f32[16,256,128]{2,1,0:T(8,128)} %convolution_bitcast_fusion), calls=%async_computation.2 | async-start | bytes 4194304 | tf_op jit(solution)/shard_map/all_to_all | solution.py:29
  354.6 28.5 %copy-start.1 = (f32[1,256,128]{2,1,0:T(8,128)S(1)}, f32[1,256,128]{2,1,0:T(8,128)}, u32[]{:S(2)}) copy-start(f32[1,256,128]{2,1,0:T(8,128)} %param.12) | copy-start | bytes 393220
Sparse Core Ops, SparseCore 0:
  122.8 141.4 all-reduce.2
  281.1 60.5 reduce-scatter.1
